TPU v7x, 256 devices: a whole 4x4x8 slice. The times are simulated.
256 devices in a mesh: tm: 32 (over y, z), space: 8 (over x, core).
Axes of the slice: x: 4, y: 4, z: 8, core: 2. Of those that a mesh axis runs over, the one named last changes fastest.
Arguments:
- inverse_factor: bfloat16 [2, 32, 4096, 4096], P(None, 'tm', 'space'), may hold values from -1.5 to 1.5, as said below
- tile_mask: int32 [32, 32], replicated, may hold values 0 or 1
- carry_rate: float32 [32, 4096, 2], P('tm', 'space'), may hold values from 0 to 1
- right_side: float32 [32, 4096, 2, 128], P('tm', 'space'), may hold values from -1.5 to 1.5
- arrow_rows: bfloat16 [32, 4096, 2, 512], P('tm', 'space'), may hold values from -0.0625 to 0.0625
- fixed_rhs: float32 [2, 512, 128], P(None, ('tm', 'space')), may hold values from -6 to 6
- tip_factor: bfloat16 [2, 512, 512], replicated, may hold values from -1 to 1, as said below
Outputs:
- solution: float32 [32, 4096, 2, 128], P('tm', 'space')
- fixed_solution: float32 [2, 512, 128], P(None, ('tm', 'space'))
Inputs may be any that keep to these rules, and one draw needn't show every extreme that they name: `tile_mask`: 1 marks a tile that may be nonzero. `inverse_factor`: only entries on or below the diagonal are read. `tip_factor`: only entries on or below the diagonal are read.
All inputs are finite; a program needn't handle non-finite values.
Results may differ from a plain program's by a relative error of at most 0.022.
Values may be sent and summed in bfloat16 or wider, within the bound.
No kernel may reach another device: no remote copies, remote signals or barrier semaphores. Data moves between devices by JAX's collectives and lax.ppermute only.
A program may use at most 320 MiB of HBM per device.

v0:
```python
import jax
import jax.numpy as jnp
from jax import lax
from jax.sharding import PartitionSpec as P

TILE = 128


def carried_in(shard, axis, join, neutral, backward):
    count = lax.axis_size(axis)
    place = lax.axis_index(axis)
    ahead = count - 1 - place if backward else place
    gathered = jax.tree.map(
        lambda a, kind: lax.all_gather(a.astype(kind), axis), shard, (jnp.bfloat16, jnp.bfloat16)
    )
    state = jax.tree.map(lambda a, e: jnp.zeros_like(a) + jnp.asarray(e, a.dtype), shard, neutral)

    def one(turn, state):
        source = count - 1 - turn if backward else turn
        return join(
            state,
            jax.tree.map(
                lambda a, own: lax.dynamic_index_in_dim(a, source, 0, False).astype(own.dtype),
                gathered,
                shard,
            ),
        )

    return lax.fori_loop(0, ahead, one, state)


def combine(earlier, latter):
    rate_new = latter[0] * earlier[0]
    rest = tuple(
        (value_l + latter[0] * value_e for value_l, value_e in zip(latter[1:], earlier[1:]))
    )
    return (rate_new,) + rest


def tile_keep(tile_table, row_start, row_total, col_total):
    tile_count = tile_table.shape[0]
    tile_ids = jnp.arange(tile_count, dtype=jnp.int32)
    row_index = row_start + jnp.arange(row_total, dtype=jnp.int32)
    col_index = jnp.arange(col_total, dtype=jnp.int32)
    row_onehot = (row_index[:, None] // TILE == tile_ids[None, :]).astype(jnp.float32)
    col_onehot = (col_index[:, None] // TILE == tile_ids[None, :]).astype(jnp.float32)
    marked = jnp.dot(jnp.dot(row_onehot, tile_table.astype(jnp.float32)), col_onehot.T)
    return (marked > 0.5) & (row_index[:, None] >= col_index[None, :])


def on_device(inverse_factor, tile_mask, carry_rate, right_side, arrow_rows, fixed_rhs, tip_factor):
    row_count = right_side.shape[1]
    node_total = inverse_factor.shape[3]
    row_start = lax.axis_index("space") * row_count
    tile_table = jnp.maximum(tile_mask, jnp.eye(tile_mask.shape[0], dtype=jnp.int32))
    weights = inverse_factor[:, 0]
    bf_zero = jnp.zeros((), jnp.bfloat16)
    rate_col = carry_rate[0][:, :, None]
    source = right_side[0]
    unit_rate = jnp.ones_like(rate_col)
    earlier_sum = carried_in(
        (rate_col, source), "tm", combine, (unit_rate, jnp.zeros_like(source)), False
    )
    forward = source + rate_col * earlier_sum[1]
    forward_b = forward.astype(jnp.bfloat16)
    row_keep = tile_keep(tile_table, row_start, row_count, node_total)
    masked_rows = jnp.where(row_keep[None], weights, bf_zero)
    block = masked_rows
    inner_rows = jnp.einsum(
        "hrn,nhk->rhk",
        block,
        lax.all_gather(forward_b, "space", axis=0, tiled=True),
        preferred_element_type=jnp.float32,
    ).astype(jnp.bfloat16)
    block = masked_rows
    scaled = lax.psum_scatter(
        jnp.einsum("hrn,rhk->nhk", block, inner_rows, preferred_element_type=jnp.float32).astype(
            jnp.bfloat16
        ),
        "space",
        scatter_dimension=0,
        tiled=True,
    ).astype(jnp.float32)
    arrow_part = arrow_rows[0]
    coupling = jnp.einsum("rhf,rhk->hfk", arrow_part, forward_b, preferred_element_type=jnp.float32)
    share_rows = fixed_rhs.shape[1]
    share_start = lax.axis_index(("tm", "space")) * share_rows
    contrib = -coupling
    own_part = lax.dynamic_slice_in_dim(contrib, share_start, share_rows, 1) + fixed_rhs
    contrib = lax.dynamic_update_slice_in_dim(contrib, own_part, share_start, 1)
    fixed_forward = lax.psum(contrib, ("tm", "space")).astype(jnp.bfloat16)
    fixed_total = tip_factor.shape[1]
    fixed_index = jnp.arange(fixed_total, dtype=jnp.int32)
    lower_tri = fixed_index[:, None] >= fixed_index[None, :]
    tip_lower = jnp.where(lower_tri[None], tip_factor, bf_zero)
    tip_inner = jnp.einsum(
        "hij,hjk->hik", tip_lower, fixed_forward, preferred_element_type=jnp.float32
    ).astype(jnp.bfloat16)
    fixed_solution = jnp.einsum(
        "hij,hik->hjk", tip_lower, tip_inner, preferred_element_type=jnp.float32
    )
    fixed_own = lax.dynamic_slice_in_dim(fixed_solution, share_start, share_rows, 1)
    fixed_b = fixed_solution.astype(jnp.bfloat16)
    carried = scaled - jnp.einsum(
        "rhf,hfk->rhk", arrow_part, fixed_b, preferred_element_type=jnp.float32
    )
    following = carried_in(
        (rate_col, rate_col * carried), "tm", combine, (unit_rate, jnp.zeros_like(carried)), True
    )
    solution = carried + following[1]
    return (solution[None], fixed_own)


def solution(mesh):
    placed = (
        P(None, "tm", "space", None),
        P(),
        P("tm", "space", None),
        P("tm", "space", None, None),
        P("tm", "space", None, None),
        P(None, ("tm", "space"), None),
        P(),
    )
    return jax.shard_map(
        on_device,
        mesh=mesh,
        in_specs=placed,
        out_specs=(P("tm", "space", None, None), P(None, ("tm", "space"), None)),
        check_vma=False,
    )
```

profile of v0, /device:TPU:2, one launch (start us, length us, event | category | flops | bytes accessed | tf_op | source)
XLA Modules:
  0.0 596.0 jit_solution(12626880782622736189)
XLA Ops:
  11.1 52.1 %all-gather = bf16[32,512,2]{1,2,0:T(2,128)(2,1)S(1)} all-gather(bf16[1,512,2]{1,2,0:T(2,128)(2,1)S(1)} %convert_element_type.103), channel_id=2, replica_groups=mesh['tm'=32,'space'=8] {'tm'}, dimensions={0}, use_global_device_ids=true | all-gather | bytes 67584 | tf_op jit(solution)/shard_map/all_gather | solution.py:14
  63.2 3.3 copy.37
  66.6 46.1 %all-gather.6.cloned.1.call-done = bf16[32,512,2,128]{3,1,2,0:T(8,128)(2,1)} async-done(((bf16[1,512,2,128]{3,1,2,0:T(8,128)(2,1)}), bf16[32,512,2,128]{3,1,2,0:T(8,128)(2,1)}) %all-gather.6.cloned.1.call-update) | async-done | bytes 8388624 | tf_op jit(solution)/shard_map/all_gather | solution.py:14
  114.4 4.2 fusion
  118.6 154.2 %all-gather.8.cloned.1.call-done = bf16[4096,2,128]{0,2,1:T(8,128)(2,1)} async-done(((bf16[512,2,128]{0,2,1:T(8,128)(2,1)}), bf16[4096,2,128]{0,2,1:T(8,128)(2,1)}) %all-gather.8.cloned.1.call-update) | async-done | bytes 2097168 | tf_op jit(solution)/shard_map/all_gather | solution.py:72
  272.7 13.2 %fusion.4 = bf16[4096,2,128]{0,2,1:T(8,128)(2,1)} fusion(bf16[2,1,512,4096]{3,2,1,0:T(8,128)(2,1)} %param.11, pred[512,4096]{1,0:T(8,128)(4,1)} %fusion, bf16[4096,2,128]{0,2,1:T(8,128)(2,1)} %all-gather.8.cloned.1.call-done), kind=kOutput, calls=%fused_computation.12 | convolution fusion | flops 2157051904 | bytes 14680064 | tf_op jit(solution)/shard_map/hrn,rhk->nhk/dot_general | solution.py:77
  287.8 78.9 %all-reduce.1 = bf16[2,512,128]{1,2,0:T(8,128)(2,1)S(1)} all-reduce(f32[2,512,128]{1,2,0:T(8,128)S(1)} %dynamic_update_slice.3), channel_id=1, replica_groups=mesh['tm'=32,'space'=8] {'tm','space'}, use_global_device_ids=true, to_apply=%region_3.4 | all-reduce | flops 131072 | bytes 786432 | tf_op jit(solution)/shard_map/psum | solution.py:91
  366.7 2.3 fusion.9
  369.0 2.1 multiply_convert_fusion
  371.8 102.9 %all-gather.10.cloned.1.call-done = bf16[16384,2,128]{0,2,1:T(8,128)(2,1)} async-done(((bf16[512,2,128]{0,2,1:T(8,128)(2,1)}), bf16[16384,2,128]{0,2,1:T(8,128)(2,1)}) %all-gather.10.cloned.1.call-update) | async-done | bytes 8388624 | tf_op jit(solution)/shard_map/all_gather | solution.py:14
  474.7 21.1 %copy.52 = bf16[16384,2,128]{2,1,0:T(2,128)(2,1)} copy(bf16[16384,2,128]{0,2,1:T(8,128)(2,1)} %all-gather.10.cloned.1.call-done) | data formatting | bytes 16777216 | tf_op jit(solution)/shard_map/while | solution.py:29
  495.9 92.2 %while.27 = (s32[]{:T(128)}, f32[512,2,128]{2,1,0:T(2,128)S(1)}, s32[]{:T(128)}, bf16[32,512,2,128]{3,2,1,0:T(2,128)(2,1)}, bf16[32,512,2,1]{2,1,3,0:T(8,128)(2,...) while((s32[]{:T(128)}, f32[512,2,128]{2,1,0:T(2,128)S(1)}, s32[]{:T(128)}, ...), condition=%wide.region_5.6_spmd, body=%wide.region_4.5_spmd.sunk | while | flops 394246 | bytes 1321107 | solution.py:29
  499.8 2.0 convert_add_fusion.5
  502.8 2.0 convert_add_fusion.5
  505.8 2.0 convert_add_fusion.5
  508.8 2.0 convert_add_fusion.5
  511.7 2.0 convert_add_fusion.5
  520.7 2.0 convert_add_fusion.5
  523.6 2.0 convert_add_fusion.5
  526.6 2.0 convert_add_fusion.5
  529.6 2.0 convert_add_fusion.5
  538.5 2.0 convert_add_fusion.5
  541.5 2.0 convert_add_fusion.5
  544.5 2.0 convert_add_fusion.5
  547.4 2.0 convert_add_fusion.5
  556.3 2.0 convert_add_fusion.5
  559.3 2.0 convert_add_fusion.5
  562.3 2.0 convert_add_fusion.5
  565.3 2.0 convert_add_fusion.5
  568.2 2.0 convert_add_fusion.5
  577.2 2.0 convert_add_fusion.5
  580.1 2.0 convert_add_fusion.5
  (80 shorter events, 60.3 us)
Async XLA Ops:
  7.2 279.1 %copy-start = (bf16[1,512,2,512]{3,2,1,0:T(2,128)(2,1)S(1)}, bf16[1,512,2,512]{3,2,1,0:T(2,128)(2,1)}, u32[]{:S(2)}) copy-start(bf16[1,512,2,512]{3,2,1,0:T(2,128)(2,1)} %param.15) | copy-start | bytes 3145732
  7.2 105.5 %all-gather.6.cloned.1.call-start = ((), (), s32[]{:S(2)}) async-start(), calls=%async_computation.1 | async-start | bytes 8650752 | tf_op jit(solution)/shard_map/all_gather | solution.py:14
  9.1 263.6 %all-gather.8.cloned.1.call-start = ((), (), s32[]{:S(2)}) async-start(), calls=%async_computation.2 | async-start | bytes 2359296 | tf_op jit(solution)/shard_map/all_gather | solution.py:72
  112.8 0.7 copy-start.2
  112.8 1.6 copy-start.4
  114.3 254.7 %reduce-scatter.2.cloned.1.call-start = ((), (), s32[]{:S(2)}) async-start(), calls=%async_computation.3 | async-start | bytes 2359296 | tf_op jit(solution)/shard_map/reduce_scatter | solution.py:76
  118.6 167.5 %copy-start.3 = (f32[2,2,128]{2,1,0:T(2,128)S(1)}, f32[2,2,128]{2,1,0:T(2,128)}, u32[]{:S(2)}) copy-start(f32[2,2,128]{2,1,0:T(2,128)} %param.16) | copy-start | bytes 6148
  118.6 167.7 %copy-start.1 = (bf16[512,2,128]{0,2,1:T(8,128)(2,1)S(1)}, bf16[512,2,128]{0,2,1:T(8,128)(2,1)}, u32[]{:S(2)}) copy-start(bf16[512,2,128]{0,2,1:T(8,128)(2,1)} %fusion.19) | copy-start | bytes 786436
  286.0 188.7 %all-gather.10.cloned.1.call-start = ((), (), s32[]{:S(2)}) async-start(), calls=%async_computation.4 | async-start | bytes 8650752 | tf_op jit(solution)/shard_map/all_gather | solution.py:14
Sparse Core Ops, SparseCore 0:
  11.2 101.4 all-gather.5
  115.0 157.6 all-gather.7
  286.1 34.6 reduce-scatter.1
  371.3 103.2 all-gather.9
where the time goes:
time: 598 us; the launch traced here: 596 us
  waiting for transfers between devices  303 us (51%)
  blocking collectives  131 us (22%)
  other arithmetic  92.9 us (16%)
  local copies, waits for them, and re-layouts  31.4 us (5%)
  matrix products  22.2 us (4%)
  between operations  14 us (2%)
    all_gather x1, waiting for transfers between devices, on_device(): lax.all_gather(forward_b, 'space', axis=0, tiled=True)  154 us
    all_gather x2, waiting for transfers between devices, carried_in(): lax.all_gather(a.astype(kind), axis)  149 us
    psum x1, blocking collectives, on_device(): fixed_forward = lax.psum(contrib, ('tm', 'space')).astype(jnp.bfloat16)  78.9 us
    add x31, other arithmetic, combine(): value_l + latter[0] * value_e  62.3 us
    all_gather x1, blocking collectives, carried_in(): lax.all_gather(a.astype(kind), axis)  52.1 us
    convert_element_type x31, other arithmetic, one(): lax.dynamic_index_in_dim(a, source, 0, False).astype(own.dtype)  28.8 us
    while x4, local copies, waits for them, and re-layouts, carried_in(): return lax.fori_loop(0, ahead, one, state)  24.8 us
    dot_general x1, matrix products, on_device(): jnp.einsum('hrn,rhk->nhk', block, inner_rows, preferred_element_type=jnp....  13.2 us
  transfers between devices with their start and end apart: 4, of which 3 were waited for; matrix products, arithmetic and copies ran while one was open for 2% of the time, Pallas kernels for 0%

commit v1 on v0

--- a/solution.py
+++ b/solution.py
@@ -88,7 +88,8 @@
     contrib = -coupling
     own_part = lax.dynamic_slice_in_dim(contrib, share_start, share_rows, 1) + fixed_rhs
     contrib = lax.dynamic_update_slice_in_dim(contrib, own_part, share_start, 1)
-    fixed_forward = lax.psum(contrib, ("tm", "space")).astype(jnp.bfloat16)
+    heads_test = lambda array_in: jax.lax.psum(jax.lax.psum(array_in, "tm"), "space")
+    fixed_forward = heads_test(contrib).astype(jnp.bfloat16)
     fixed_total = tip_factor.shape[1]
     fixed_index = jnp.arange(fixed_total, dtype=jnp.int32)
     lower_tri = fixed_index[:, None] >= fixed_index[None, :]

time: 598 us -> 691 us (1.16)
  waiting for transfers between devices: 303 us -> 446 us
  blocking collectives: 131 us -> 79.5 us
    psum x0 -> x1, waiting for transfers between devices: none -> 139 us  [on_device(): jax.lax.psum(array_in, 'tm')]
    psum x1, blocking collectives: 78.9 us -> 27.4 us  [on_device(): jax.lax.psum(jax.lax.psum(array_in, 'tm'), 'space')]
  transfers between devices with their start and end apart: 4 -> 5, of which waited for: 3 -> 5; matrix products, arithmetic and copies ran while one was open for 2% -> 4% of each run, Pallas kernels for 0% -> 0%
where the time goes in v1:
time: 691 us; the launch traced here: 689 us
  waiting for transfers between devices  446 us (65%)
  other arithmetic  92.9 us (13%)
  blocking collectives  79.5 us (12%)
  local copies, waits for them, and re-layouts  32.3 us (5%)
  matrix products  22.4 us (3%)
  between operations  14 us (2%)
    all_gather x2, waiting for transfers between devices, carried_in(): lax.all_gather(a.astype(kind), axis)  153 us
    all_gather x1, waiting for transfers between devices, on_device(): lax.all_gather(forward_b, 'space', axis=0, tiled=True)  152 us
    psum x1, waiting for transfers between devices, on_device(): jax.lax.psum(array_in, 'tm')  139 us
    add x31, other arithmetic, combine(): value_l + latter[0] * value_e  62.3 us
    all_gather x1, blocking collectives, carried_in(): lax.all_gather(a.astype(kind), axis)  52.1 us
    convert_element_type x31, other arithmetic, one(): lax.dynamic_index_in_dim(a, source, 0, False).astype(own.dtype)  28.8 us
    psum x1, blocking collectives, on_device(): jax.lax.psum(jax.lax.psum(array_in, 'tm'), 'space')  27.4 us
    while x4, local copies, waits for them, and re-layouts, carried_in(): return lax.fori_loop(0, ahead, one, state)  24.9 us
  transfers between devices with their start and end apart: 5, of which 5 were waited for; matrix products, arithmetic and copies ran while one was open for 4% of the time, Pallas kernels for 0%

profile of v1, /device:TPU:2, one launch (start us, length us, event | category | flops | bytes accessed | tf_op | source)
XLA Modules:
  0.0 688.8 jit_solution(10983389347193668959)
XLA Ops:
  11.1 52.1 %all-gather = bf16[32,512,2]{1,2,0:T(2,128)(2,1)S(1)} all-gather(bf16[1,512,2]{1,2,0:T(2,128)(2,1)S(1)} %convert_element_type.103), channel_id=2, replica_groups=mesh['tm'=32,'space'=8] {'tm'}, dimensions={0}, use_global_device_ids=true | all-gather | bytes 67584 | tf_op jit(solution)/shard_map/all_gather | solution.py:14
  63.2 3.3 copy.37
  66.6 46.1 %all-gather.6.cloned.1.call-done = bf16[32,512,2,128]{3,1,2,0:T(8,128)(2,1)} async-done(((bf16[1,512,2,128]{3,1,2,0:T(8,128)(2,1)}), bf16[32,512,2,128]{3,1,2,0:T(8,128)(2,1)}) %all-gather.6.cloned.1.call-update) | async-done | bytes 8388624 | tf_op jit(solution)/shard_map/all_gather | solution.py:14
  114.6 4.2 fusion
  121.1 151.6 %all-gather.8.cloned.1.call-done = bf16[4096,2,128]{0,2,1:T(8,128)(2,1)} async-done(((bf16[512,2,128]{0,2,1:T(8,128)(2,1)}), bf16[4096,2,128]{0,2,1:T(8,128)(2,1)}) %all-gather.8.cloned.1.call-update) | async-done | bytes 2097168 | tf_op jit(solution)/shard_map/all_gather | solution.py:72
  272.7 13.4 %fusion.4 = bf16[4096,2,128]{0,2,1:T(8,128)(2,1)} fusion(bf16[2,1,512,4096]{3,2,1,0:T(8,128)(2,1)} %param.11, pred[512,4096]{1,0:T(8,128)(4,1)} %fusion, bf16[4096,2,128]{0,2,1:T(8,128)(2,1)} %all-gather.8.cloned.1.call-done), kind=kOutput, calls=%fused_computation.12 | convolution fusion | flops 2157051904 | bytes 14680064 | tf_op jit(solution)/shard_map/hrn,rhk->nhk/dot_general | solution.py:77
  286.3 139.2 %all-reduce.3.cloned.1.call-done = f32[2,512,128]{1,2,0:T(8,128)} async-done(((f32[2,512,128]{1,2,0:T(8,128)}), f32[2,512,128]{1,2,0:T(8,128)}) %all-reduce.3.cloned.1.call-update) | async-done | bytes 524304 | tf_op jit(solution)/shard_map/psum | solution.py:91
  425.5 27.4 %all-reduce.4 = bf16[2,512,128]{1,2,0:T(8,128)(2,1)S(1)} all-reduce(f32[2,512,128]{1,2,0:T(8,128)} %all-reduce.3.cloned.1.call-done), channel_id=1, replica_groups=mesh['tm'=32,'space'=8] {'space'}, use_global_device_ids=true, to_apply=%region_4.5 | all-reduce | flops 131072 | bytes 786432 | tf_op jit(solution)/shard_map/psum | solution.py:91
  452.9 2.3 fusion.9
  455.3 3.0 reduce-scatter.2.cloned.1.call-done
  458.3 2.1 multiply_convert_fusion
  461.0 106.4 %all-gather.10.cloned.1.call-done = bf16[16384,2,128]{0,2,1:T(8,128)(2,1)} async-done(((bf16[512,2,128]{0,2,1:T(8,128)(2,1)}), bf16[16384,2,128]{0,2,1:T(8,128)(2,1)}) %all-gather.10.cloned.1.call-update) | async-done | bytes 8388624 | tf_op jit(solution)/shard_map/all_gather | solution.py:14
  567.5 21.1 %copy.52 = bf16[16384,2,128]{2,1,0:T(2,128)(2,1)} copy(bf16[16384,2,128]{0,2,1:T(8,128)(2,1)} %all-gather.10.cloned.1.call-done) | data formatting | bytes 16777216 | tf_op jit(solution)/shard_map/while | solution.py:29
  588.7 92.2 %while.27 = (s32[]{:T(128)}, f32[512,2,128]{2,1,0:T(2,128)S(1)}, s32[]{:T(128)}, bf16[32,512,2,128]{3,2,1,0:T(2,128)(2,1)}, bf16[32,512,2,1]{2,1,3,0:T(8,128)(2,...) while((s32[]{:T(128)}, f32[512,2,128]{2,1,0:T(2,128)S(1)}, s32[]{:T(128)}, ...), condition=%wide.region_6.7_spmd, body=%wide.region_5.6_spmd.sunk | while | flops 394246 | bytes 1321107 | solution.py:29
  595.6 2.0 convert_add_fusion.5
  598.6 2.0 convert_add_fusion.5
  601.6 2.0 convert_add_fusion.5
  604.6 2.0 convert_add_fusion.5
  613.5 2.0 convert_add_fusion.5
  616.5 2.0 convert_add_fusion.5
  619.4 2.0 convert_add_fusion.5
  622.4 2.0 convert_add_fusion.5
  631.3 2.0 convert_add_fusion.5
  634.3 2.0 convert_add_fusion.5
  637.3 2.0 convert_add_fusion.5
  640.3 2.0 convert_add_fusion.5
  643.2 2.0 convert_add_fusion.5
  652.2 2.0 convert_add_fusion.5
  655.1 2.0 convert_add_fusion.5
  658.1 2.0 convert_add_fusion.5
  661.1 2.0 convert_add_fusion.5
  670.0 2.0 convert_add_fusion.5
  (85 shorter events, 65.1 us)
Async XLA Ops:
  7.2 111.6 %copy-start = (bf16[1,512,2,512]{3,2,1,0:T(2,128)(2,1)S(1)}, bf16[1,512,2,512]{3,2,1,0:T(2,128)(2,1)}, u32[]{:S(2)}) copy-start(bf16[1,512,2,512]{3,2,1,0:T(2,128)(2,1)} %param.15) | copy-start | bytes 3145732
  7.2 105.5 %all-gather.6.cloned.1.call-start = ((), (), s32[]{:S(2)}) async-start(), calls=%async_computation.1 | async-start | bytes 8650752 | tf_op jit(solution)/shard_map/all_gather | solution.py:14
  9.1 263.6 %all-gather.8.cloned.1.call-start = ((), (), s32[]{:S(2)}) async-start(), calls=%async_computation.2 | async-start | bytes 2359296 | tf_op jit(solution)/shard_map/all_gather | solution.py:72
  112.8 0.7 copy-start.3
  112.8 1.6 copy-start.4
  112.8 1.7 copy-start.5
  114.3 311.2 %all-reduce.3.cloned.1.call-start = ((), (), s32[]{:S(2)}) async-start(), calls=%async_computation.4 | async-start | bytes 1048576 | tf_op jit(solution)/shard_map/psum | solution.py:91
  114.5 4.2 copy-start.2
  120.2 0.8 copy-start.1
  121.1 337.2 %reduce-scatter.2.cloned.1.call-start = ((), (), s32[]{:S(2)}) async-start(), calls=%async_computation.3 | async-start | bytes 2359296 | tf_op jit(solution)/shard_map/reduce_scatter | solution.py:76
  286.1 281.3 %all-gather.10.cloned.1.call-start = ((), (), s32[]{:S(2)}) async-start(), calls=%async_computation.5 | async-start | bytes 8650752 | tf_op jit(solution)/shard_map/all_gather | solution.py:14
Sparse Core Ops, SparseCore 0:
  11.2 101.4 all-gather.5
  114.5 158.2 all-gather.7
  276.7 148.7 all-reduce.2
  428.1 30.1 reduce-scatter.1
  461.5 105.9 all-gather.9
